TPU v7x, 256 devices: a 8x8x2 block of a 8x8x16 slice. The times are simulated.
256 devices in a mesh: grp: 2 (over z), tp: 128 (over y, x, core).
Axes of the slice: x: 8, y: 8, z: 2, core: 2. Of those that a mesh axis runs over, the one named last changes fastest.
The devices are a block of a 8x8x16 slice.
Arguments:
- hidden: bfloat16 [1024, 16384], P('grp', 'tp'), parts along dimension 0, may hold values from -36 to 36
- norm_gain: float32 [16384], P('tp'), may hold values from 0.3 to 10, as said below
- prefix: int32 [2], P('grp'), parts along dimension 0, may hold values from 0 to 8192
- w_query: bfloat16 [16384, 16384], P(None, 'tp'), may hold values from -0.046875 to 0.046875
- w_kv: bfloat16 [2048, 16384], P('tp'), may hold values from -0.046875 to 0.046875
- w_scale: float32 [18432], P('tp'), may hold values from 0.25 to 4
Outputs:
- queries: bfloat16 [1024, 16384], P('grp', 'tp'), parts along dimension 0
- keys: bfloat16 [1024, 16384], P('grp', 'tp'), parts along dimension 0
- values: bfloat16 [1024, 16384], P('grp', 'tp'), parts along dimension 0
- payload: bfloat16 [1024, 16384], P('grp', 'tp'), parts along dimension 0
- row_scale: float32 [1024], P('grp'), parts along dimension 0
There are 2 independent parts, one for each index of `grp`. A program takes and returns all parts, laid end to end along the dimension named above; an argument that names none is the same for every part. Nothing has to cross between parts.
Inputs may be any that keep to these rules, and one draw needn't show every extreme that they name: `norm_gain`: positive.
All inputs are finite; a program needn't handle non-finite values. Where the computation divides by a largest or mean magnitude, that divisor is 1e-20 or more.
Results may differ from a plain program's by a relative error of at most 0.012.
Values may be sent and summed in bfloat16 or wider, within the bound.
A program may use at most 64 MiB of HBM per device.

v0:
```python
import jax
import jax.numpy as jnp
from jax import lax
from jax.sharding import PartitionSpec as P

D = 16384
HD = 128
HQ_DEV = 1
KV_COLS_DEV = 8
norm_eps = 1e-05
tiny_eps = 1e-06
rope_base = 500000.0


def turned_gather(arrays, axis, dims):
    turned = [jnp.moveaxis(a, dim, 0) for a, dim in zip(arrays, dims)]
    widths = [t[0].size for t in turned]
    both = jnp.concatenate([t.reshape(-1, w) for t, w in zip(turned, widths)], axis=1)
    whole = lax.all_gather(both, axis, axis=0, tiled=True)
    blocks = jnp.split(whole, [sum(widths[:k]) for k in range(1, len(widths))], axis=1)
    return tuple(
        (
            jnp.moveaxis(b.reshape(-1, *t.shape[1:]), 0, dim)
            for b, t, dim in zip(blocks, turned, dims)
        )
    )


def rotate(matrix, positions, offset):
    count, width = matrix.shape
    pairs = matrix.reshape(count, width // 2, 2)
    columns = offset + 2 * jnp.arange(width // 2, dtype=jnp.int32)
    pair_index = (columns % HD // 2).astype(jnp.float32)
    inverse_freq = jnp.power(jnp.float32(rope_base), -(2.0 * pair_index) / HD)
    angle = positions.astype(jnp.float32)[:, None] * inverse_freq[None, :]
    cosine = jnp.cos(angle)
    sine = jnp.sin(angle)
    first = pairs[:, :, 0]
    second = pairs[:, :, 1]
    turned = jnp.stack([first * cosine - second * sine, second * cosine + first * sine], axis=-1)
    return turned.reshape(count, width)


def kv_product(left, right_rows):
    return lax.dot_general(
        left, right_rows, (((1,), (1,)), ((), ())), preferred_element_type=jnp.float32
    )


def pick_head(gathered, head, kv_heads):
    count = gathered.shape[0]
    pieces = gathered.shape[1] // (kv_heads * KV_COLS_DEV)
    grouped = gathered.reshape(count, pieces, kv_heads, KV_COLS_DEV)
    chosen = lax.dynamic_slice_in_dim(grouped, head, 1, 2)
    return chosen.reshape(count, pieces * KV_COLS_DEV)


def local(hidden, norm_gain, prefix, w_query, w_kv, w_scale):
    count = hidden.shape[0]
    local_width = hidden.shape[1]
    whole, gains = (
        lax.all_gather(hidden, "tp", axis=1, tiled=True),
        lax.all_gather(norm_gain[None, :].astype(jnp.bfloat16), "tp", axis=1, tiled=True).astype(
            jnp.float32
        ),
    )
    widened = whole.astype(jnp.float32)
    square_sum = jnp.sum(widened * widened, axis=1)
    inverse = 1.0 / jnp.sqrt(square_sum / D + norm_eps)
    normed = widened * gains * inverse[:, None]
    row_scale = jnp.max(jnp.abs(normed), axis=1) + tiny_eps
    full_payload = (normed / row_scale[:, None]).astype(jnp.bfloat16)
    payload = lax.dynamic_slice_in_dim(
        full_payload, lax.axis_index("tp") * local_width, local_width, 1
    )
    query_raw = jnp.dot(full_payload, w_query, preferred_element_type=jnp.float32)
    kv_raw = kv_product(full_payload, w_kv)
    proj = jnp.concatenate([query_raw, kv_raw], axis=1)
    proj = proj * row_scale[:, None] * w_scale[None, :]
    qwidth = HQ_DEV * HD
    query_cols = proj[:, :qwidth]
    key_cols = proj[:, qwidth : qwidth + KV_COLS_DEV]
    value_cols = proj[:, qwidth + KV_COLS_DEV :]
    kv_heads = KV_COLS_DEV * lax.axis_size("tp") // HD
    my_index = lax.axis_index("tp")
    positions = prefix[0] + jnp.arange(count, dtype=jnp.int32)
    queries = rotate(query_cols, positions, 0).astype(jnp.bfloat16)
    rotated_keys = rotate(key_cols, positions, my_index // kv_heads * KV_COLS_DEV).astype(
        jnp.bfloat16
    )
    value_round = value_cols.astype(jnp.bfloat16)
    all_keys, all_values = turned_gather((rotated_keys, value_round), "tp", (1, 1))
    head = my_index * kv_heads // lax.axis_size("tp")
    key_head = pick_head(all_keys, head, kv_heads)
    value_head = pick_head(all_values, head, kv_heads)
    keys = jnp.tile(key_head, (1, HQ_DEV))
    values = jnp.tile(value_head, (1, HQ_DEV))
    return (queries, keys, values, payload, row_scale)


def solution(mesh):
    return jax.shard_map(
        local,
        mesh=mesh,
        in_specs=(P("grp", "tp"), P("tp"), P("grp"), P(None, "tp"), P("tp", None), P("tp")),
        out_specs=(P("grp", "tp"), P("grp", "tp"), P("grp", "tp"), P("grp", "tp"), P("grp")),
        check_vma=False,
    )
```

profile of v0, /device:TPU:513, one launch (start us, length us, event | category | flops | bytes accessed | tf_op | source)
XLA Modules:
  0.0 265.4 jit_solution(17900371330747141451)
XLA Ops:
  7.2 0.0 copy-start
  7.2 0.1 all-gather.5.cloned.1.call-start
  7.3 0.7 all-gather.5.cloned.1.call-update
  8.0 0.1 all-gather.7.cloned.1.call-start
  8.1 0.7 convert_bitcast_fusion
  8.7 58.2 %all-gather.1 = bf16[128,1,128]{2,1,0:T(2,128)(2,1)S(1)} all-gather(bf16[1,1,128]{2,1,0:T(2,128)(2,1)S(1)} %convert_bitcast_fusion), channel_id=2, replica_groups=mesh['grp'=2,'tp'=128] {'tp'}, dimensions={0}, use_global_device_ids=true | all-gather | bytes 33024 | tf_op jit(solution)/shard_map/all_gather | solution.py:63
  66.9 0.1 mul.199
  67.7 68.7 %all-gather.5.cloned.1.call-done = bf16[512,16384]{1,0:T(8,128)(2,1)} async-done(((bf16[512,128]{1,0:T(8,128)(2,1)}), bf16[512,16384]{1,0:T(8,128)(2,1)}) %all-gather.5.cloned.1.call-update) | async-done | bytes 16777232 | tf_op jit(solution)/shard_map/all_gather | solution.py:62
  136.3 0.0 copy-start.2
  136.3 7.4 %fusion.5 = f32[512]{0:T(512)S(1)} fusion(bf16[512,16384]{1,0:T(8,128)(2,1)} %all-gather.5.cloned.1.call-done), kind=kLoop, calls=%fused_computation.7 | loop fusion | flops 25165312 | bytes 16779264 | tf_op jit(solution)/shard_map/reduce_sum | solution.py:68
  143.8 3.2 %copy-done.2 = bf16[512,16384]{1,0:T(8,128)(2,1)S(1)} copy-done((bf16[512,16384]{1,0:T(8,128)(2,1)S(1)}, bf16[512,16384]{1,0:T(8,128)(2,1)}, u32[]{:S(2)}) %copy-start.2) | copy-done | bytes 16777240
  147.0 6.2 %fusion.3 = f32[512]{0:T(512)S(1)} fusion(bf16[512,16384]{1,0:T(8,128)(2,1)S(1)} %copy-done.2, f32[16384]{0:T(1024)S(1)} %bitcast.36, f32[512]{0:T(512)S(1)} %add_rsqrt_fusion), kind=kLoop, calls=%fused_computation.5 | loop fusion | flops 41942528 | bytes 16846848 | tf_op jit(solution)/shard_map/reduce_max | solution.py:71
  153.2 0.0 copy-start.4
  153.2 5.5 %fusion.4 = bf16[512,16384]{1,0:T(8,128)(2,1)S(1)} fusion(bf16[512,16384]{1,0:T(8,128)(2,1)S(1)} %copy-done.2, f32[16384]{0:T(1024)S(1)} %bitcast.37, f32[512]{0:T(512)S(1)} %broadcast_add_fusion, f32[512]{0:T(512)S(1)} %add_rsqrt_fusion), kind=kLoop, calls=%fused_computation.6 | loop fusion | flops 41943040 | bytes 33624064 | tf_op jit(solution)/shard_map/convert_element_type | solution.py:72
  158.7 0.0 copy-start.1
  158.7 5.7 %copy-done.1 = bf16[512,16384]{1,0:T(8,128)(2,1)} copy-done((bf16[512,16384]{1,0:T(8,128)(2,1)}, bf16[512,16384]{1,0:T(8,128)(2,1)S(1)}, u32[]{:S(2)}) %copy-start.1) | copy-done | bytes 16777240
  164.5 0.0 copy-done
  164.5 0.0 copy-start.3
  164.5 0.0 copy-start.5
  164.5 4.4 %fusion.30 = f32[512,16]{0,1:T(8,128)S(1)} fusion(bf16[512,16384]{1,0:T(8,128)(2,1)S(1)} %fusion.4, bf16[16,16384]{1,0:T(8,128)(2,1)S(1)} %copy-done), kind=kOutput, calls=%fused_computation.64 | convolution fusion | flops 268435456 | bytes 17334272 | tf_op jit(solution)/shard_map/dot_general | solution.py:45
  168.9 0.0 copy-done.3
  168.9 9.3 %fusion.29 = f32[512,128]{0,1:T(8,128)S(1)} fusion(bf16[512,16384]{1,0:T(8,128)(2,1)} %copy-done.1, bf16[16384,128]{1,0:T(8,128)(2,1)S(1)} %copy-done.3), kind=kOutput, calls=%fused_computation.63 | convolution fusion | flops 2147483648 | bytes 21233664 | tf_op jit(solution)/shard_map/dot_general | solution.py:76
  178.2 0.0 copy-done.4
  178.2 0.0 copy-done.5
  178.2 0.1 fusion.6
  178.3 0.1 fusion.20
  178.5 0.6 pad_maximum_fusion.1
  179.1 0.1 all-gather.7.cloned.1.call-update
  179.3 0.1 reshape.290
  179.4 0.2 fusion.27
  179.6 0.6 fusion.12
  180.2 0.1 copy.32
  180.4 0.1 convert_element_type.50
  180.4 0.8 copy.38
  181.2 1.6 constant_dynamic-slice_fusion
  182.8 72.5 %all-gather.7.cloned.1.call-done = bf16[1024,1024]{1,0:T(8,128)(2,1)} async-done(((bf16[8,1024]{1,0:T(8,128)(2,1)}), bf16[1024,1024]{1,0:T(8,128)(2,1)}) %all-gather.7.cloned.1.call-update) | async-done | bytes 2097168 | tf_op jit(solution)/shard_map/all_gather | solution.py:19
  255.3 1.7 fusion.26
  257.0 0.8 copy.39
  257.7 0.8 copy.40
  (15 shorter events, 0.2 us)
Async XLA Ops:
  7.2 157.3 %copy-start = (bf16[16,16384]{1,0:T(8,128)(2,1)S(1)}, bf16[16,16384]{1,0:T(8,128)(2,1)}, u32[]{:S(2)}) copy-start(bf16[16,16384]{1,0:T(8,128)(2,1)} %param.10) | copy-start | bytes 1572868
  7.2 129.1 %all-gather.5.cloned.1.call-start = ((), (), s32[]{:S(2)}) async-start(), calls=%async_computation | async-start | bytes 16908288 | tf_op jit(solution)/shard_map/all_gather | solution.py:62
  8.0 247.3 %all-gather.7.cloned.1.call-start = ((), (), s32[]{:S(2)}) async-start(), calls=%async_computation.1 | async-start | bytes 2113536 | tf_op jit(solution)/shard_map/all_gather | solution.py:19
  136.3 10.7 %copy-start.2 = (bf16[512,16384]{1,0:T(8,128)(2,1)S(1)}, bf16[512,16384]{1,0:T(8,128)(2,1)}, u32[]{:S(2)}) copy-start(bf16[512,16384]{1,0:T(8,128)(2,1)} %all-gather.5.cloned.1.call-done) | copy-start | bytes 50331652
  153.2 24.9 %copy-start.4 = (f32[512]{0:T(512)}, f32[512]{0:T(512)S(1)}, u32[]{:S(2)}) copy-start(f32[512]{0:T(512)S(1)} %broadcast_add_fusion) | copy-start | bytes 6148
  158.7 5.7 %copy-start.1 = (bf16[512,16384]{1,0:T(8,128)(2,1)}, bf16[512,16384]{1,0:T(8,128)(2,1)S(1)}, u32[]{:S(2)}) copy-start(bf16[512,16384]{1,0:T(8,128)(2,1)S(1)} %fusion.4) | copy-start | bytes 50331652
  164.5 4.4 %copy-start.3 = (bf16[16384,128]{1,0:T(8,128)(2,1)S(1)}, bf16[16384,128]{1,0:T(8,128)(2,1)}, u32[]{:S(2)}) copy-start(bf16[16384,128]{1,0:T(8,128)(2,1)} %param.9) | copy-start | bytes 12582916
  164.5 13.7 %copy-start.5 = (f32[144]{0:T(256)S(1)}, f32[144]{0:T(256)}, u32[]{:S(2)}) copy-start(f32[144]{0:T(256)} %param.11) | copy-start | bytes 1732
Sparse Core Ops, SparseCore 0:
  10.5 125.7 all-gather.4
  179.3 75.8 all-gather.6
where the time goes:
time: 266 us; the launch traced here: 265 us
  waiting for transfers between devices  142 us (53%)
  blocking collectives  58.2 us (22%)
  other arithmetic  21.4 us (8%)
  local copies, waits for them, and re-layouts  15.1 us (6%)
  between operations  15 us (6%)
  matrix products  13.7 us (5%)
    all_gather x1, waiting for transfers between devices, turned_gather(): whole = lax.all_gather(both, axis, axis=0, tiled=True)  72.5 us
    all_gather x1, waiting for transfers between devices, local(): lax.all_gather(hidden, 'tp', axis=1, tiled=True)  68.7 us
    all_gather x1, blocking collectives, local(): lax.all_gather(norm_gain[None, :].astype(jnp.bfloat16), 'tp', axis=1, til...  58.2 us
    unnamed x15, local copies, waits for them, and re-layouts  11.2 us
    dot_general x1, matrix products, local(): jnp.dot(full_payload, w_query, preferred_element_type=jnp.float32)  9.25 us
    reduce_sum x1, other arithmetic, local(): square_sum = jnp.sum(widened * widened, axis=1)  7.43 us
    reduce_max x1, other arithmetic, local(): row_scale = jnp.max(jnp.abs(normed), axis=1) + tiny_eps  6.23 us
    convert_element_type x1, other arithmetic, local(): full_payload = (normed / row_scale[:, None]).astype(jnp.bfloat16)  5.48 us
  transfers between devices with their start and end apart: 2, of which 2 were waited for; matrix products, arithmetic and copies ran while one was open for 2% of the time, Pallas kernels for 0%

commit v1 on v0

--- a/solution.py
+++ b/solution.py
@@ -16,7 +16,9 @@
     turned = [jnp.moveaxis(a, dim, 0) for a, dim in zip(arrays, dims)]
     widths = [t[0].size for t in turned]
     both = jnp.concatenate([t.reshape(-1, w) for t, w in zip(turned, widths)], axis=1)
-    whole = lax.all_gather(both, axis, axis=0, tiled=True)
+    whole = jnp.concatenate(
+        lax.all_to_all(jnp.stack([both] * lax.axis_size(axis)), axis, 0, 0), axis=0
+    )
     blocks = jnp.split(whole, [sum(widths[:k]) for k in range(1, len(widths))], axis=1)
     return tuple(
         (

time: 266 us -> 251 us (0.944)
  waiting for transfers between devices: 142 us -> 116 us
  starting transfers between devices: 0.12 us -> 10.5 us
    all_gather x1 -> x0, waiting for transfers between devices: 72.5 us -> none  [turned_gather(): whole = lax.all_gather(both, axis, axis=0, tiled=True)]
    all_to_all x0 -> x1, waiting for transfers between devices: none -> 47 us  [turned_gather(): lax.all_to_all(jnp.stack([both] * lax.axis_size(axis)), axis, 0, 0)]
    all_to_all x0 -> x1, starting transfers between devices: none -> 10.5 us  [turned_gather(): lax.all_to_all(jnp.stack([both] * lax.axis_size(axis)), axis, 0, 0)]
where the time goes in v1:
time: 251 us; the launch traced here: 250 us
  waiting for transfers between devices  116 us (46%)
  blocking collectives  58.2 us (23%)
  other arithmetic  20.8 us (8%)
  local copies, waits for them, and re-layouts  15.2 us (6%)
  between operations  15 us (6%)
  matrix products  13.7 us (5%)
  starting transfers between devices  10.5 us (4%)
    all_gather x1, waiting for transfers between devices, local(): lax.all_gather(hidden, 'tp', axis=1, tiled=True)  68.7 us
    all_gather x1, blocking collectives, local(): lax.all_gather(norm_gain[None, :].astype(jnp.bfloat16), 'tp', axis=1, til...  58.2 us
    all_to_all x1, waiting for transfers between devices, turned_gather(): lax.all_to_all(jnp.stack([both] * lax.axis_size(axis)), axis, 0, 0)  47 us
    unnamed x15, local copies, waits for them, and re-layouts  11.2 us
    all_to_all x1, starting transfers between devices, turned_gather(): lax.all_to_all(jnp.stack([both] * lax.axis_size(axis)), axis, 0, 0)  10.5 us
    dot_general x1, matrix products, local(): jnp.dot(full_payload, w_query, preferred_element_type=jnp.float32)  9.26 us
    reduce_sum x1, other arithmetic, local(): square_sum = jnp.sum(widened * widened, axis=1)  7.43 us
    reduce_max x1, other arithmetic, local(): row_scale = jnp.max(jnp.abs(normed), axis=1) + tiny_eps  6.23 us
  transfers between devices with their start and end apart: 2, of which 2 were waited for; matrix products, arithmetic and copies ran while one was open for 2% of the time, Pallas kernels for 0%

profile of v1, /device:TPU:513, one launch (start us, length us, event | category | flops | bytes accessed | tf_op | source)
XLA Modules:
  0.0 249.7 jit_solution(6166466555624683161)
XLA Ops:
  7.2 0.0 copy-start
  7.2 0.1 all-gather.4.cloned.1.call-start
  7.3 0.7 all-gather.4.cloned.1.call-update
  8.0 0.7 convert_bitcast_fusion
  8.7 58.2 %all-gather.1 = bf16[128,1,128]{2,1,0:T(2,128)(2,1)S(1)} all-gather(bf16[1,1,128]{2,1,0:T(2,128)(2,1)S(1)} %convert_bitcast_fusion), channel_id=2, replica_groups=mesh['grp'=2,'tp'=128] {'tp'}, dimensions={0}, use_global_device_ids=true | all-gather | bytes 33024 | tf_op jit(solution)/shard_map/all_gather | solution.py:65
  66.9 0.1 mul.199
  67.6 68.7 %all-gather.4.cloned.1.call-done = bf16[512,16384]{1,0:T(8,128)(2,1)} async-done(((bf16[512,128]{1,0:T(8,128)(2,1)}), bf16[512,16384]{1,0:T(8,128)(2,1)}) %all-gather.4.cloned.1.call-update) | async-done | bytes 16777232 | tf_op jit(solution)/shard_map/all_gather | solution.py:64
  136.3 0.0 copy-start.2
  136.3 7.4 %fusion.5 = f32[512]{0:T(512)S(1)} fusion(bf16[512,16384]{1,0:T(8,128)(2,1)} %all-gather.4.cloned.1.call-done), kind=kLoop, calls=%fused_computation.7 | loop fusion | flops 25165312 | bytes 16779264 | tf_op jit(solution)/shard_map/reduce_sum | solution.py:70
  143.8 3.2 %copy-done.2 = bf16[512,16384]{1,0:T(8,128)(2,1)S(1)} copy-done((bf16[512,16384]{1,0:T(8,128)(2,1)S(1)}, bf16[512,16384]{1,0:T(8,128)(2,1)}, u32[]{:S(2)}) %copy-start.2) | copy-done | bytes 16777240
  147.0 6.2 %fusion.3 = f32[512]{0:T(512)S(1)} fusion(bf16[512,16384]{1,0:T(8,128)(2,1)S(1)} %copy-done.2, f32[16384]{0:T(1024)S(1)} %bitcast.34, f32[512]{0:T(512)S(1)} %add_rsqrt_fusion), kind=kLoop, calls=%fused_computation.5 | loop fusion | flops 41942528 | bytes 16846848 | tf_op jit(solution)/shard_map/reduce_max | solution.py:73
  153.2 0.0 copy-start.4
  153.2 5.5 %fusion.4 = bf16[512,16384]{1,0:T(8,128)(2,1)S(1)} fusion(bf16[512,16384]{1,0:T(8,128)(2,1)S(1)} %copy-done.2, f32[16384]{0:T(1024)S(1)} %bitcast.35, f32[512]{0:T(512)S(1)} %broadcast_add_fusion, f32[512]{0:T(512)S(1)} %add_rsqrt_fusion), kind=kLoop, calls=%fused_computation.6 | loop fusion | flops 41943040 | bytes 33624064 | tf_op jit(solution)/shard_map/convert_element_type | solution.py:74
  158.7 0.0 copy-start.1
  158.7 5.7 %copy-done.1 = bf16[512,16384]{1,0:T(8,128)(2,1)} copy-done((bf16[512,16384]{1,0:T(8,128)(2,1)}, bf16[512,16384]{1,0:T(8,128)(2,1)S(1)}, u32[]{:S(2)}) %copy-start.1) | copy-done | bytes 16777240
  164.5 0.0 copy-done
  164.5 0.0 copy-start.3
  164.5 0.0 copy-start.5
  164.5 4.4 %fusion.30 = f32[512,16]{0,1:T(8,128)S(1)} fusion(bf16[512,16384]{1,0:T(8,128)(2,1)S(1)} %fusion.4, bf16[16,16384]{1,0:T(8,128)(2,1)S(1)} %copy-done), kind=kOutput, calls=%fused_computation.64 | convolution fusion | flops 268435456 | bytes 17334272 | tf_op jit(solution)/shard_map/dot_general | solution.py:47
  168.9 0.0 copy-done.3
  168.9 9.3 %fusion.29 = f32[512,128]{0,1:T(8,128)S(1)} fusion(bf16[512,16384]{1,0:T(8,128)(2,1)} %copy-done.1, bf16[16384,128]{1,0:T(8,128)(2,1)S(1)} %copy-done.3), kind=kOutput, calls=%fused_computation.63 | convolution fusion | flops 2147483648 | bytes 21233664 | tf_op jit(solution)/shard_map/dot_general | solution.py:78
  178.2 0.0 copy-done.4
  178.2 0.0 copy-done.5
  178.2 0.1 fusion.6
  178.3 0.1 fusion.20
  178.6 1.6 stack.10
  180.2 10.5 %all-to-all-start = ((bf16[128,8,1024]{2,1,0:T(8,128)(2,1)}), bf16[128,8,1024]{2,1,0:T(8,128)(2,1)S(1)}, u32[]{:S(2)}, u32[]{:S(2)}) async-start(bf16[128,8,1024]{2,1,0:T(8,128)(2,1)} %stack.10), calls=%async_computation | async-start | bytes 4194304 | tf_op jit(solution)/shard_map/all_to_all | solution.py:20
  190.7 0.1 reshape.295
  190.8 0.2 fusion.27
  191.1 0.6 fusion.12
  191.7 0.1 copy.24
  191.8 0.1 convert_element_type.50
  191.9 0.8 copy.28
  192.6 1.6 constant_dynamic-slice_fusion
  194.2 47.0 %all-to-all-done = bf16[128,8,1024]{2,1,0:T(8,128)(2,1)S(1)} async-done(((bf16[128,8,1024]{2,1,0:T(8,128)(2,1)}), bf16[128,8,1024]{2,1,0:T(8,128)(2,1)S(1)}, u32[]{:S(2)}, u32[]{:S(2)}) %all-to-all-start) | async-done | bytes 2097184 | tf_op jit(solution)/shard_map/all_to_all | solution.py:20
  241.2 0.2 fusion.26
  241.4 0.8 copy.29
  242.1 0.8 copy.30
  (16 shorter events, 0.2 us)
Async XLA Ops:
  7.2 157.3 %copy-start = (bf16[16,16384]{1,0:T(8,128)(2,1)S(1)}, bf16[16,16384]{1,0:T(8,128)(2,1)}, u32[]{:S(2)}) copy-start(bf16[16,16384]{1,0:T(8,128)(2,1)} %param.10) | copy-start | bytes 1572868
  7.2 129.1 %all-gather.4.cloned.1.call-start = ((), (), s32[]{:S(2)}) async-start(), calls=%async_computation.1 | async-start | bytes 16908288 | tf_op jit(solution)/shard_map/all_gather | solution.py:64
  136.3 10.7 %copy-start.2 = (bf16[512,16384]{1,0:T(8,128)(2,1)S(1)}, bf16[512,16384]{1,0:T(8,128)(2,1)}, u32[]{:S(2)}) copy-start(bf16[512,16384]{1,0:T(8,128)(2,1)} %all-gather.4.cloned.1.call-done) | copy-start | bytes 50331652
  153.2 24.9 %copy-start.4 = (f32[512]{0:T(512)}, f32[512]{0:T(512)S(1)}, u32[]{:S(2)}) copy-start(f32[512]{0:T(512)S(1)} %broadcast_add_fusion) | copy-start | bytes 6148
  158.7 5.7 %copy-start.1 = (bf16[512,16384]{1,0:T(8,128)(2,1)}, bf16[512,16384]{1,0:T(8,128)(2,1)S(1)}, u32[]{:S(2)}) copy-start(bf16[512,16384]{1,0:T(8,128)(2,1)S(1)} %fusion.4) | copy-start | bytes 50331652
  164.5 4.4 %copy-start.3 = (bf16[16384,128]{1,0:T(8,128)(2,1)S(1)}, bf16[16384,128]{1,0:T(8,128)(2,1)}, u32[]{:S(2)}) copy-start(bf16[16384,128]{1,0:T(8,128)(2,1)} %param.9) | copy-start | bytes 12582916
  164.5 13.7 %copy-start.5 = (f32[144]{0:T(256)S(1)}, f32[144]{0:T(256)}, u32[]{:S(2)}) copy-start(f32[144]{0:T(256)} %param.11) | copy-start | bytes 1732
  180.2 61.0 %all-to-all-start = ((bf16[128,8,1024]{2,1,0:T(8,128)(2,1)}), bf16[128,8,1024]{2,1,0:T(8,128)(2,1)S(1)}, u32[]{:S(2)}, u32[]{:S(2)}) async-start(bf16[128,8,1024]{2,1,0:T(8,128)(2,1)} %stack.10), calls=%async_computation | async-start | bytes 4194304 | tf_op jit(solution)/shard_map/all_to_all | solution.py:20
Sparse Core Ops, SparseCore 0:
  10.5 125.7 all-gather.3
